TPU v7x, 256 devices: a whole 4x4x8 slice. The times are simulated.
256 devices in a mesh: outer: 8 (over y, core), inner: 32 (over z, x).
Axes of the slice: x: 4, y: 4, z: 8, core: 2. Of those that a mesh axis runs over, the one named last changes fastest.
Arguments:
- tokens: bfloat16 [98304, 4096], P(('outer', 'inner')), may hold values from -6 to 6
- out_grad: bfloat16 [98304, 1024], P(('outer', 'inner')), may hold values from -0.25 to 0.25
- master_weights: float32 [1024, 4096], P(('outer', 'inner')), may hold values from -0.0421 to 0.0421
- base_weights: bfloat16 [1024, 4096], replicated, may hold values from -0.030029297 to 0.030029297
- adam_m: float32 [1024, 4096], P(('outer', 'inner')), may hold values from -8 to 8
- adam_v: float32 [1024, 4096], P(('outer', 'inner')), may hold values from 0.1 to 10
- grad_exps: int32 [256, 8, 32], P(('outer', 'inner')), may hold values from -13 to -8
- diff_exps: int32 [1024, 32], P(('outer', 'inner')), may hold values from -20 to -15
- hadamard_signs: int32 [32, 128], replicated, may hold values 0 or 1
Outputs:
- projected: bfloat16 [98304, 1024], P(('outer', 'inner'))
- new_master: float32 [1024, 4096], P(('outer', 'inner'))
- new_first: float32 [1024, 4096], P(('outer', 'inner'))
- new_second: float32 [1024, 4096], P(('outer', 'inner'))
All inputs are finite; a program needn't handle non-finite values.
Results may differ from a plain program's by a relative error of at most 0.005.
Values may be sent and summed in bfloat16 or wider, within the bound.
No kernel may reach another device: no remote copies, remote signals or barrier semaphores. Data moves between devices by JAX's collectives and lax.ppermute only.
A program may use at most 128 MiB of HBM per device.

v0:
```python
import math
import jax
import jax.numpy as jnp
from jax import lax
from jax.sharding import Mesh
from jax.sharding import PartitionSpec as P

ADAM_STEP = 10
INNER = ("inner_0", "inner_1")
OUTER_INNER = ("outer", "inner_0", "inner_1")
clip_level = 448.0
beta_one = 0.9
beta_two = 0.95
learn_rate = 0.002
decay_rate = 0.1
adam_eps = 1e-08
highest = lax.Precision.HIGHEST


def summed_rows(terms, axes):
    running = terms.astype(jnp.bfloat16)
    for axis in axes:
        running = lax.psum_scatter(running, axis, scatter_dimension=0, tiled=True)
    return running.astype(jnp.float32)


def in_blocks(value, dim, count):
    before, after = (value.shape[:dim], value.shape[dim + 1 :])
    return jnp.moveaxis(value.reshape(*before, count, -1, *after), dim, 0)


def sum_at_owner(value, axis, dim):
    count = lax.axis_size(axis)
    blocks = lax.all_to_all(in_blocks(value, dim, count), axis, 0, 0, tiled=True)
    return jnp.sum(blocks.astype(jnp.float32), axis=0)


def sent_to_all(value, axis):
    count = lax.axis_size(axis)
    return lax.all_to_all(
        jnp.broadcast_to(value[None], (count, *value.shape)), axis, 0, 0, tiled=True
    )


def joined_along(blocks, dim):
    blocks = jnp.moveaxis(blocks, 0, dim)
    dims = blocks.shape
    return blocks.reshape(*dims[:dim], dims[dim] * dims[dim + 1], *dims[dim + 2 :])


def gathered_copies(value, axis, dim):
    blocks = sent_to_all(value, axis)
    return joined_along(blocks, dim)


def hadamard(matrix_size):
    positions = jnp.arange(matrix_size, dtype=jnp.int32)
    common = positions[:, None] & positions[None, :]
    parity = jnp.zeros((matrix_size, matrix_size), jnp.int32)
    for bit_level in range(matrix_size.bit_length() - 1):
        parity = parity + (common >> bit_level & 1)
    return (1 - 2 * (parity % 2)).astype(jnp.float32)


def rotate_rows(row_block, sign_rows, matrix):
    row_count = row_block.shape[0]
    blocks = row_block.reshape(row_count, sign_rows.shape[0], sign_rows.shape[1]) * sign_rows
    turned = jnp.dot(blocks.reshape(-1, sign_rows.shape[1]), matrix, precision=highest)
    return turned.reshape(row_block.shape) / math.sqrt(sign_rows.shape[1])


def unrotate_rows(row_block, sign_rows, matrix):
    row_count = row_block.shape[0]
    turned = jnp.dot(
        row_block.reshape(-1, sign_rows.shape[1]), matrix, precision=highest
    ) / math.sqrt(sign_rows.shape[1])
    return (turned.reshape(row_count, sign_rows.shape[0], sign_rows.shape[1]) * sign_rows).reshape(
        row_block.shape
    )


def clip_rows(row_block, bound_rows):
    row_count = row_block.shape[0]
    shaped = row_block.reshape(row_count, bound_rows.shape[1], -1)
    limits = bound_rows[:, :, None]
    return jnp.clip(shaped, -limits, limits).reshape(row_block.shape)


def adam_update(gradient, master, first, second):
    new_first = beta_one * first + (1.0 - beta_one) * gradient
    new_second = beta_two * second + (1.0 - beta_two) * gradient * gradient
    fix_one = 1.0 - beta_one**ADAM_STEP
    fix_two = 1.0 - beta_two**ADAM_STEP
    step_dir = new_first / fix_one / (jnp.sqrt(new_second / fix_two) + adam_eps)
    new_master = master - learn_rate * (step_dir + decay_rate * master)
    return (new_master, new_first, new_second)


def shards(
    tokens,
    out_grad,
    master_weights,
    base_weights,
    adam_m,
    adam_v,
    grad_exps,
    diff_exps,
    hadamard_signs,
):
    outer_count = lax.axis_size("outer")
    inner_count = lax.axis_size(INNER)
    token_rows = tokens.shape[0]
    model_width = tokens.shape[1]
    rows_dev = master_weights.shape[0]
    sign_rows = (2 * hadamard_signs - 1).astype(jnp.float32)
    block_len = sign_rows.shape[1]
    col_blocks = sign_rows.shape[0]
    matrix = hadamard(block_len)
    bound_all = jnp.repeat(
        clip_level * jnp.exp2(grad_exps[0].astype(jnp.float32)), block_len, axis=0
    )
    grad_grid = out_grad.reshape(token_rows, outer_count, inner_count, rows_dev).transpose(
        0, 2, 1, 3
    )
    bound_grid = bound_all.reshape(outer_count, inner_count, rows_dev, col_blocks).transpose(
        1, 0, 2, 3
    )
    coded_bound_sel = bound_grid.reshape(-1, col_blocks)
    term_rows = lax.dot_general(
        grad_grid.reshape(token_rows, -1),
        tokens,
        (((0,), (0,)), ((), ())),
        preferred_element_type=jnp.float32,
    )
    turned = rotate_rows(term_rows, sign_rows, matrix)
    coded_rows = lax.optimization_barrier(clip_rows(turned, coded_bound_sel).astype(jnp.bfloat16))
    coded_rows = coded_rows.astype(jnp.float32)
    group_sum = summed_rows(
        coded_rows.reshape(1 * lax.axis_size(INNER), outer_count, rows_dev, model_width), INNER
    )
    summed = sum_at_owner(group_sum.astype(jnp.bfloat16), "outer", 1).reshape(rows_dev, model_width)
    gradient = unrotate_rows(summed, sign_rows, matrix)
    new_master, new_first, new_second = adam_update(gradient, master_weights, adam_m, adam_v)
    owner = lax.axis_index("outer") * inner_count + lax.axis_index(INNER)
    base_own = lax.dynamic_slice_in_dim(base_weights, owner * rows_dev, rows_dev, 0).astype(
        jnp.float32
    )
    diff_bound = clip_level * jnp.exp2(diff_exps.astype(jnp.float32))
    diff_coded = clip_rows(new_master - base_own, diff_bound).astype(jnp.bfloat16)
    outer_part = gathered_copies(diff_coded.reshape(1, 1, rows_dev, model_width), "outer", 0)
    base_grid = base_weights.reshape(outer_count, inner_count, rows_dev, model_width)
    effective = (
        base_grid.astype(jnp.float32)
        + lax.all_gather(outer_part, INNER, axis=1, tiled=True).astype(jnp.float32)
    ).astype(jnp.bfloat16)
    result = lax.dot_general(
        tokens, effective, (((1,), (3,)), ((), ())), preferred_element_type=jnp.float32
    )
    projected = (
        result.reshape(token_rows, outer_count, -1).astype(jnp.bfloat16).reshape(token_rows, -1)
    )
    return (projected, new_master, new_first, new_second)


def solution(mesh):
    split = Mesh(mesh.devices.reshape(mesh.shape["outer"], 8, 4), ("outer", "inner_0", "inner_1"))
    return jax.shard_map(
        shards,
        mesh=split,
        in_specs=(
            P(OUTER_INNER, None),
            P(OUTER_INNER, None),
            P(OUTER_INNER, None),
            P(),
            P(OUTER_INNER, None),
            P(OUTER_INNER, None),
            P(OUTER_INNER, None, None),
            P(OUTER_INNER, None),
            P(),
        ),
        out_specs=(
            P(OUTER_INNER, None),
            P(OUTER_INNER, None),
            P(OUTER_INNER, None),
            P(OUTER_INNER, None),
        ),
        check_vma=False,
    )
```

profile of v0, /device:TPU:1, one launch (start us, length us, event | category | flops | bytes accessed | tf_op | source)
XLA Modules:
  0.0 408.4 jit_solution(3144663483152369432)
XLA Ops:
  7.9 3.4 copy.50
  11.4 2.3 copy.38
  13.7 2.4 reshape.73
  16.0 2.3 copy.39
  18.3 2.3 reshape.81
  20.6 5.7 %convolution_multiply_fusion.1 = f32[1024,32,128]{2,0,1:T(8,128)S(1)} fusion(bf16[384,1024,1]{0,1,2:T(8,128)(2,1)} %reshape.81, bf16[32,128,384]{2,1,0:T(8,128)(2,1)S(1)} %bitcast.61, f32[32,128]{1,0:T(8,128)S(1)} %get-tuple-element.25), kind=kOutput, calls=%fused_computation.6 | convolution fusion | flops 3225419776 | bytes 20725760 | tf_op jit(solution)/shard_map/dot_general | solution.py:129
  26.3 20.2 %copy.41 = f32[1024,32,128]{2,1,0:T(8,128)S(1)} copy(f32[1024,32,128]{2,0,1:T(8,128)S(1)} %convolution_multiply_fusion.1) | data formatting | bytes 33554432 | tf_op jit(solution)/shard_map/mul | solution.py:67
  46.4 15.3 %convolution_multiply_fusion = bf16[32768,128]{1,0:T(8,128)(2,1)} fusion(f32[32768,128]{1,0:T(8,128)S(1)} %bitcast.56), kind=kOutput, calls=%fused_computation | convolution fusion | flops 6451412992 | bytes 25165824 | tf_op jit(solution)/shard_map/dot_general | solution.py:68
  61.8 13.4 %div.31 = bf16[1024,4096]{1,0:T(8,128)(2,1)} reshape(bf16[32768,128]{1,0:T(8,128)(2,1)} %convolution_multiply_fusion) | data formatting | bytes 16777216 | tf_op jit(solution)/shard_map/div | solution.py:69
  75.3 11.7 %max.32 = bf16[1024,32,128]{2,1,0:T(8,128)(2,1)S(1)} broadcast(bf16[1024,32]{1,0:T(8,128)(2,1)S(1)} %neg.13), dimensions={0,1} | broadcast | bytes 8454144 | tf_op jit(solution)/shard_map/jit(clip)/max | solution.py:86
  87.1 10.2 %min.35 = bf16[1024,32,128]{2,1,0:T(8,128)(2,1)S(1)} broadcast(f32[1024,32]{1,0:T(8,128)S(1)} %bitcast.63), dimensions={0,1} | broadcast | bytes 8519680 | tf_op jit(solution)/shard_map/jit(clip)/min | solution.py:86
  97.3 6.5 %fusion.1 = bf16[1024,4096]{1,0:T(8,128)(2,1)} fusion(bf16[1024,4096]{1,0:T(8,128)(2,1)S(1)} %bitcast.58, bf16[128,8,32,128]{3,2,1,0:T(8,128)(2,1)S(1)} %bitcast.59, bf16[128,8,32,128]{3,2,1,0:T(8,128)(2,1)S(1)} %bitcast.60), kind=kLoop, calls=%fused_computation.3 | loop fusion | flops 8388608 | bytes 33554432 | tf_op jit(solution)/shard_map/convert_element_type | solution.py:136
  103.8 13.1 %convert_element_type.63 = bf16[32,8,4,4096]{3,2,1,0:T(4,128)(2,1)} reshape(bf16[1024,4096]{1,0:T(8,128)(2,1)} %fusion.1) | data formatting | bytes 16777216 | tf_op jit(solution)/shard_map/convert_element_type | solution.py:21
  117.0 15.5 %copy.42 = bf16[32,8,4,4096]{3,1,2,0:T(8,128)(2,1)} copy(bf16[32,8,4,4096]{3,2,1,0:T(4,128)(2,1)} %convert_element_type.63) | data formatting | bytes 16777216 | tf_op jit(solution)/shard_map/convert_element_type | solution.py:21
  132.7 98.6 %reduce-scatter.3.cloned.1.call-done = bf16[4,8,4,4096]{3,1,2,0:T(8,128)(2,1)} async-done(((bf16[32,8,4,4096]{3,1,2,0:T(8,128)(2,1)}), bf16[4,8,4,4096]{3,1,2,0:T(8,128)(2,1)}) %reduce-scatter.3.cloned.1.call-update) | async-done | bytes 1048592 | tf_op jit(solution)/shard_map/reduce_scatter | solution.py:23
  231.4 25.8 %reduce-scatter.5.cloned.1.call-done = bf16[1,8,4,4096]{3,1,2,0:T(8,128)(2,1)} async-done(((bf16[4,8,4,4096]{3,1,2,0:T(8,128)(2,1)}), bf16[1,8,4,4096]{3,1,2,0:T(8,128)(2,1)}) %reduce-scatter.5.cloned.1.call-update) | async-done | bytes 262160 | tf_op jit(solution)/shard_map/reduce_scatter | solution.py:23
  257.3 1.9 copy.43
  259.1 6.3 %all-to-all-start = ((bf16[8,1,1,4,4096]{4,3,2,1,0:T(4,128)(2,1)}), bf16[8,1,1,4,4096]{4,3,2,1,0:T(4,128)(2,1)S(1)}, u32[]{:S(2)}, u32[]{:S(2)}) async-start(bf16[8,1,1,4,4096]{4,3,2,1,0:T(4,128)(2,1)} %copy.43), calls=%async_computation.2 | async-start | bytes 524288 | tf_op jit(solution)/shard_map/all_to_all | solution.py:34
  265.5 6.4 %all-to-all-done = bf16[8,1,1,4,4096]{4,3,2,1,0:T(4,128)(2,1)S(1)} async-done(((bf16[8,1,1,4,4096]{4,3,2,1,0:T(4,128)(2,1)}), bf16[8,1,1,4,4096]{4,3,2,1,0:T(4,128)(2,1)S(1)}, u32[]{:S(2)}, u32[]{:S(2)}) %all-to-all-start) | async-done | bytes 262176 | tf_op jit(solution)/shard_map/all_to_all | solution.py:34
  274.2 9.9 %all_to_all.10 = bf16[8,1,1,4,4096]{4,3,2,1,0:T(4,128)(2,1)S(1)} all-to-all(bf16[8,1,1,4,4096]{4,3,2,1,0:T(4,128)(2,1)S(1)} %broadcast_in_dim.2), channel_id=1, replica_groups=mesh['outer'=8,'inner_0'=8,'inner_1'=4] {'outer'}, dimensions={0} | all-to-all | bytes 524288 | tf_op jit(solution)/shard_map/all_to_all | solution.py:40
  285.0 15.5 %reshape.78 = f32[8,32,4,4096]{3,2,1,0:T(4,128)} reshape(bf16[1024,4096]{1,0:T(8,128)(2,1)} %param.12) | data formatting | bytes 25165824 | tf_op jit(solution)/shard_map/convert_element_type | solution.py:153
  300.5 80.9 %all-gather.3.cloned.1.call-done = bf16[8,32,1,4,4096]{4,0,3,2,1:T(8,128)(2,1)} async-done(((bf16[8,1,1,4,4096]{4,0,3,2,1:T(8,128)(2,1)}), bf16[8,32,1,4,4096]{4,0,3,2,1:T(8,128)(2,1)}) %all-gather.3.cloned.1.call-update) | async-done | bytes 8388624 | tf_op jit(solution)/shard_map/all_gather | solution.py:154
  381.4 13.8 %fusion.2 = bf16[8,32,4,4096]{3,2,1,0:T(4,128)(2,1)S(1)} fusion(f32[8,32,4,4096]{3,2,1,0:T(4,128)} %reshape.78, bf16[8,32,1,4,4096]{4,0,3,2,1:T(8,128)(2,1)} %all-gather.3.cloned.1.call-done), kind=kLoop, calls=%fused_computation.5 | loop fusion | flops 12582912 | bytes 33554432 | tf_op jit(solution)/shard_map/convert_element_type | solution.py:155
  395.2 5.0 %fusion.11 = bf16[384,8,32,4]{0,1,3,2:T(8,128)(2,1)S(1)} fusion(bf16[384,4096]{1,0:T(8,128)(2,1)S(1)} %copy-done, bf16[8,32,4,4096]{3,2,1,0:T(4,128)(2,1)S(1)} %fusion.2), kind=kOutput, calls=%fused_computation.11 | convolution fusion | flops 3221618688 | bytes 12320768 | tf_op jit(solution)/shard_map/dot_general | solution.py:156
  (39 shorter events, 6.1 us)
Async XLA Ops:
  7.2 224.2 %reduce-scatter.3.cloned.1.call-start = ((), (), s32[]{:S(2)}) async-start(), calls=%async_computation.4 | async-start | bytes 9437184 | tf_op jit(solution)/shard_map/reduce_scatter | solution.py:23
  61.8 13.4 %copy-start.4 = (s32[1,8,32]{2,1,0:T(8,128)S(1)}, s32[1,8,32]{2,1,0:T(8,128)}, u32[]{:S(2)}) copy-start(s32[1,8,32]{2,1,0:T(8,128)} %param.15) | copy-start | bytes 3076
  75.3 22.0 %slice-start = ((s8[8388608]{0:T(1024)(128)(4,1)}), s8[4194304]{0:T(1024)(128)(4,1)S(1)}, s32[]{:S(2)}) async-start(s8[8388608]{0:T(1024)(128)(4,1)} %bitcast.57), calls=%async_computation.7 | async-start | bytes 8388608
  87.1 10.3 %slice-start.1 = ((s8[8388608]{0:T(1024)(128)(4,1)}), s8[4194304]{0:T(1024)(128)(4,1)S(1)}, s32[]{:S(2)}) async-start(s8[8388608]{0:T(1024)(128)(4,1)} %bitcast.57), calls=%async_computation.8 | async-start | bytes 8388608
  132.4 133.0 %copy-start.5 = (s32[4,32]{1,0:T(4,128)S(1)}, s32[4,32]{1,0:T(4,128)}, u32[]{:S(2)}) copy-start(s32[4,32]{1,0:T(4,128)} %param.16) | copy-start | bytes 1540
  132.4 140.0 %copy-start.1 = (f32[4,4096]{1,0:T(4,128)S(1)}, f32[4,4096]{1,0:T(4,128)}, u32[]{:S(2)}) copy-start(f32[4,4096]{1,0:T(4,128)} %param.11) | copy-start | bytes 196612
  132.4 140.0 %copy-start.2 = (f32[4,4096]{1,0:T(4,128)S(1)}, f32[4,4096]{1,0:T(4,128)}, u32[]{:S(2)}) copy-start(f32[4,4096]{1,0:T(4,128)} %param.13) | copy-start | bytes 196612
  132.4 140.0 %copy-start.3 = (f32[4,4096]{1,0:T(4,128)S(1)}, f32[4,4096]{1,0:T(4,128)}, u32[]{:S(2)}) copy-start(f32[4,4096]{1,0:T(4,128)} %param.14) | copy-start | bytes 196612
  132.5 124.8 %reduce-scatter.5.cloned.1.call-start = ((), (), s32[]{:S(2)}) async-start(), calls=%async_computation.5 | async-start | bytes 1310720 | tf_op jit(solution)/shard_map/reduce_scatter | solution.py:23
  259.1 12.8 %all-to-all-start = ((bf16[8,1,1,4,4096]{4,3,2,1,0:T(4,128)(2,1)}), bf16[8,1,1,4,4096]{4,3,2,1,0:T(4,128)(2,1)S(1)}, u32[]{:S(2)}, u32[]{:S(2)}) async-start(bf16[8,1,1,4,4096]{4,3,2,1,0:T(4,128)(2,1)} %copy.43), calls=%async_computation.2 | async-start | bytes 524288 | tf_op jit(solution)/shard_map/all_to_all | solution.py:34
  265.4 115.9 %all-gather.3.cloned.1.call-start = ((), (), s32[]{:S(2)}) async-start(), calls=%async_computation.6 | async-start | bytes 8650752 | tf_op jit(solution)/shard_map/all_gather | solution.py:154
  300.5 94.7 %copy-start = (bf16[384,4096]{1,0:T(8,128)(2,1)S(1)}, bf16[384,4096]{1,0:T(8,128)(2,1)}, u32[]{:S(2)}) copy-start(bf16[384,4096]{1,0:T(8,128)(2,1)} %param.9) | copy-start | bytes 9437188
Sparse Core Ops, SparseCore 0:
  132.6 98.7 reduce-scatter.2
  233.9 23.2 reduce-scatter.4
  285.1 96.2 all-gather.2
where the time goes:
time: 410 us; the launch traced here: 408 us
  waiting for transfers between devices  212 us (52%)
  local copies, waits for them, and re-layouts  117 us (29%)
  matrix products  26.3 us (6%)
  other arithmetic  22.9 us (6%)
  between operations  13.9 us (3%)
  blocking collectives  9.94 us (2%)
  starting transfers between devices  6.6 us (2%)
    reduce_scatter x2, waiting for transfers between devices, summed_rows(): running = lax.psum_scatter(running, axis, scatter_dimension=0, tiled=True)  124 us
    all_gather x1, waiting for transfers between devices, shards(): lax.all_gather(outer_part, INNER, axis=1, tiled=True).astype(jnp.float32)  80.9 us
    convert_element_type x2, local copies, waits for them, and re-layouts, summed_rows(): running = terms.astype(jnp.bfloat16)  28.6 us
    mul x1, local copies, waits for them, and re-layouts, rotate_rows(): row_block.reshape(row_count, sign_rows.shape[0], sign_rows.shape[1])  20.2 us
    convert_element_type x1, local copies, waits for them, and re-layouts, shards(): base_grid.astype(jnp.float32)  15.5 us
    dot_general x1, matrix products, rotate_rows(): jnp.dot(blocks.reshape(-1, sign_rows.shape[1]), matrix, precision=highest)  15.3 us
    convert_element_type x1, other arithmetic, shards(): effective = (base_grid.astype(jnp.float32) + lax.all_gather(outer_part, I...  13.8 us
    div x1, local copies, waits for them, and re-layouts, rotate_rows(): return turned.reshape(row_block.shape) / math.sqrt(sign_rows.shape[1])  13.4 us
  transfers between devices with their start and end apart: 4, of which 4 were waited for; matrix products, arithmetic and copies ran while one was open for 4% of the time, Pallas kernels for 0%

commit v1 on v0

--- a/solution.py
+++ b/solution.py
@@ -151,7 +151,9 @@
     base_grid = base_weights.reshape(outer_count, inner_count, rows_dev, model_width)
     effective = (
         base_grid.astype(jnp.float32)
-        + lax.all_gather(outer_part, INNER, axis=1, tiled=True).astype(jnp.float32)
+        + jnp.concatenate(
+            lax.all_to_all(jnp.stack([outer_part] * lax.axis_size(INNER)), INNER, 0, 0), axis=1
+        ).astype(jnp.float32)
     ).astype(jnp.bfloat16)
     result = lax.dot_general(
         tokens, effective, (((1,), (3,)), ((), ())), preferred_element_type=jnp.float32

time: 410 us -> 546 us (1.33)
  the two profiles are of different devices: /device:TPU:1 before, /device:TPU:118 now
where the time goes in v1:
time: 546 us; the launch traced here: 536 us
  waiting for transfers between devices  307 us (56%)
  local copies, waits for them, and re-layouts  136 us (25%)
  matrix products  44.1 us (8%)
  starting transfers between devices  15.2 us (3%)
  between operations  14.7 us (3%)
  blocking collectives  9.93 us (2%)
  other arithmetic  9.01 us (2%)
    all_to_all x1, waiting for transfers between devices, shards(): lax.all_to_all(jnp.stack([outer_part] * lax.axis_size(INNER)), INNER, 0, 0)  180 us
    reduce_scatter x2, waiting for transfers between devices, summed_rows(): running = lax.psum_scatter(running, axis, scatter_dimension=0, tiled=True)  122 us
    convert_element_type x2, local copies, waits for them, and re-layouts, summed_rows(): running = terms.astype(jnp.bfloat16)  28.6 us
    dot_general x1, matrix products, shards(): lax.dot_general(tokens, effective, (((1,), (3,)), ((), ())), preferred_el...  22.8 us
    min x1, local copies, waits for them, and re-layouts, clip_rows(): return jnp.clip(shaped, -limits, limits).reshape(row_block.shape)  21.5 us
    mul x1, local copies, waits for them, and re-layouts, rotate_rows(): row_block.reshape(row_count, sign_rows.shape[0], sign_rows.shape[1])  20.2 us
    convert_element_type x1, local copies, waits for them, and re-layouts, shards(): base_grid.astype(jnp.float32)  15.6 us
    dot_general x1, matrix products, rotate_rows(): jnp.dot(blocks.reshape(-1, sign_rows.shape[1]), matrix, precision=highest)  15.3 us
  transfers between devices with their start and end apart: 4, of which 4 were waited for; matrix products, arithmetic and copies ran while one was open for 3% of the time, Pallas kernels for 0%

profile of v1, /device:TPU:118, one launch (start us, length us, event | category | flops | bytes accessed | tf_op | source)
XLA Modules:
  0.0 536.0 jit_solution(16071557389293420566)
XLA Ops:
  7.9 3.4 copy.61
  11.4 2.3 copy.47
  13.7 2.4 reshape.78
  16.0 2.3 copy.48
  18.3 2.3 reshape.84
  20.6 5.7 %convolution_multiply_fusion.1 = f32[1024,32,128]{2,0,1:T(8,128)S(1)} fusion(bf16[384,1024,1]{0,1,2:T(8,128)(2,1)} %reshape.84, bf16[32,128,384]{2,1,0:T(8,128)(2,1)S(1)} %bitcast.63, f32[32,128]{1,0:T(8,128)S(1)} %get-tuple-element.29), kind=kOutput, calls=%fused_computation.6 | convolution fusion | flops 3225419776 | bytes 20725760 | tf_op jit(solution)/shard_map/dot_general | solution.py:129
  26.3 20.2 %copy.50 = f32[1024,32,128]{2,1,0:T(8,128)S(1)} copy(f32[1024,32,128]{2,0,1:T(8,128)S(1)} %convolution_multiply_fusion.1) | data formatting | bytes 33554432 | tf_op jit(solution)/shard_map/mul | solution.py:67
  46.5 15.3 %convolution_multiply_fusion = bf16[32768,128]{1,0:T(8,128)(2,1)} fusion(f32[32768,128]{1,0:T(8,128)S(1)} %bitcast.58), kind=kOutput, calls=%fused_computation | convolution fusion | flops 6451412992 | bytes 25165824 | tf_op jit(solution)/shard_map/dot_general | solution.py:68
  61.8 13.3 %div.31 = bf16[1024,4096]{1,0:T(8,128)(2,1)} reshape(bf16[32768,128]{1,0:T(8,128)(2,1)} %convolution_multiply_fusion) | data formatting | bytes 16777216 | tf_op jit(solution)/shard_map/div | solution.py:69
  75.3 11.7 %max.32 = bf16[1024,32,128]{2,1,0:T(8,128)(2,1)S(1)} broadcast(bf16[1024,32]{1,0:T(8,128)(2,1)S(1)} %neg.13), dimensions={0,1} | broadcast | bytes 8454144 | tf_op jit(solution)/shard_map/jit(clip)/max | solution.py:86
  87.1 21.5 %min.35 = bf16[1024,32,128]{2,1,0:T(8,128)(2,1)S(1)} broadcast(f32[1024,32]{1,0:T(8,128)S(1)} %bitcast.65), dimensions={0,1} | broadcast | bytes 8519680 | tf_op jit(solution)/shard_map/jit(clip)/min | solution.py:86
  108.6 6.5 %fusion.1 = bf16[1024,4096]{1,0:T(8,128)(2,1)} fusion(bf16[1024,4096]{1,0:T(8,128)(2,1)S(1)} %bitcast.60, bf16[128,8,32,128]{3,2,1,0:T(8,128)(2,1)S(1)} %bitcast.61, bf16[128,8,32,128]{3,2,1,0:T(8,128)(2,1)S(1)} %bitcast.62), kind=kLoop, calls=%fused_computation.3 | loop fusion | flops 8388608 | bytes 33554432 | tf_op jit(solution)/shard_map/convert_element_type | solution.py:136
  115.0 13.1 %convert_element_type.69 = bf16[32,8,4,4096]{3,2,1,0:T(4,128)(2,1)} reshape(bf16[1024,4096]{1,0:T(8,128)(2,1)} %fusion.1) | data formatting | bytes 16777216 | tf_op jit(solution)/shard_map/convert_element_type | solution.py:21
  128.2 15.5 %copy.51 = bf16[32,8,4,4096]{3,1,2,0:T(8,128)(2,1)} copy(bf16[32,8,4,4096]{3,2,1,0:T(4,128)(2,1)} %convert_element_type.69) | data formatting | bytes 16777216 | tf_op jit(solution)/shard_map/convert_element_type | solution.py:21
  143.7 96.1 %reduce-scatter.3.cloned.1.call-done = bf16[4,8,4,4096]{3,1,2,0:T(8,128)(2,1)} async-done(((bf16[32,8,4,4096]{3,1,2,0:T(8,128)(2,1)}), bf16[4,8,4,4096]{3,1,2,0:T(8,128)(2,1)}) %reduce-scatter.3.cloned.1.call-update) | async-done | bytes 1048592 | tf_op jit(solution)/shard_map/reduce_scatter | solution.py:23
  239.8 25.9 %reduce-scatter.5.cloned.1.call-done = bf16[1,8,4,4096]{3,1,2,0:T(8,128)(2,1)} async-done(((bf16[4,8,4,4096]{3,1,2,0:T(8,128)(2,1)}), bf16[1,8,4,4096]{3,1,2,0:T(8,128)(2,1)}) %reduce-scatter.5.cloned.1.call-update) | async-done | bytes 262160 | tf_op jit(solution)/shard_map/reduce_scatter | solution.py:23
  267.6 4.8 all-to-all-start
  272.5 4.3 all-to-all-done
  279.0 9.9 %all_to_all.15 = bf16[8,1,1,4,4096]{4,3,2,1,0:T(4,128)(2,1)S(1)} all-to-all(bf16[8,1,1,4,4096]{4,3,2,1,0:T(4,128)(2,1)S(1)} %broadcast_in_dim.2), channel_id=1, replica_groups=mesh['outer'=8,'inner_0'=8,'inner_1'=4] {'outer'}, dimensions={0} | all-to-all | bytes 524288 | tf_op jit(solution)/shard_map/all_to_all | solution.py:40
  289.0 7.5 %stack.3 = bf16[32,8,1,4,4096]{4,3,1,2,0:T(4,128)(2,1)} broadcast(bf16[8,4,4096]{2,1,0:T(4,128)(2,1)S(1)} %bitcast.69), dimensions={1,3,4} | broadcast | bytes 8650752 | tf_op jit(solution)/shard_map/stack | solution.py:155
  296.4 10.3 %all-to-all-start.2 = ((bf16[32,8,1,4,4096]{4,3,1,2,0:T(4,128)(2,1)}), bf16[32,8,1,4,4096]{4,3,1,2,0:T(4,128)(2,1)}, u32[]{:S(2)}, u32[]{:S(2)}) async-start(bf16[32,8,1,4,4096]{4,3,1,2,0:T(4,128)(2,1)} %stack.3), calls=%async_computation.4 | async-start | bytes 16777216 | tf_op jit(solution)/shard_map/all_to_all | solution.py:155
  306.7 15.6 %reshape.82 = f32[8,32,4,4096]{3,2,1,0:T(4,128)} reshape(bf16[1024,4096]{1,0:T(8,128)(2,1)} %param.12) | data formatting | bytes 25165824 | tf_op jit(solution)/shard_map/convert_element_type | solution.py:153
  322.3 180.4 %all-to-all-done.2 = bf16[32,8,1,4,4096]{4,3,1,2,0:T(4,128)(2,1)} async-done(((bf16[32,8,1,4,4096]{4,3,1,2,0:T(4,128)(2,1)}), bf16[32,8,1,4,4096]{4,3,1,2,0:T(4,128)(2,1)}, u32[]{:S(2)}, u32[]{:S(2)}) %all-to-all-start.2) | async-done | bytes 8388640 | tf_op jit(solution)/shard_map/all_to_all | solution.py:155
  502.7 22.8 %fusion.3 = bf16[8,32,4,384]{3,0,2,1:T(8,128)(2,1)} fusion(f32[8,32,4,4096]{3,2,1,0:T(4,128)} %reshape.82, bf16[32,8,1,4,4096]{4,3,1,2,0:T(4,128)(2,1)} %all-to-all-done.2, bf16[384,4096]{1,0:T(8,128)(2,1)S(1)} %copy-done), kind=kOutput, calls=%fused_computation.7 | convolution fusion | flops 3233808384 | bytes 29097984 | tf_op jit(solution)/shard_map/dot_general | solution.py:158
  (38 shorter events, 8.3 us)
Async XLA Ops:
  7.2 232.7 %reduce-scatter.3.cloned.1.call-start = ((), (), s32[]{:S(2)}) async-start(), calls=%async_computation.5 | async-start | bytes 9437184 | tf_op jit(solution)/shard_map/reduce_scatter | solution.py:23
  61.8 13.3 %copy-start.4 = (s32[1,8,32]{2,1,0:T(8,128)S(1)}, s32[1,8,32]{2,1,0:T(8,128)}, u32[]{:S(2)}) copy-start(s32[1,8,32]{2,1,0:T(8,128)} %param.15) | copy-start | bytes 3076
  75.3 33.3 %slice-start = ((s8[8388608]{0:T(1024)(128)(4,1)}), s8[4194304]{0:T(1024)(128)(4,1)S(1)}, s32[]{:S(2)}) async-start(s8[8388608]{0:T(1024)(128)(4,1)} %bitcast.59), calls=%async_computation.7 | async-start | bytes 8388608
  87.0 21.5 %slice-start.1 = ((s8[8388608]{0:T(1024)(128)(4,1)}), s8[4194304]{0:T(1024)(128)(4,1)S(1)}, s32[]{:S(2)}) async-start(s8[8388608]{0:T(1024)(128)(4,1)} %bitcast.59), calls=%async_computation.8 | async-start | bytes 8388608
  143.6 128.8 %copy-start.5 = (s32[4,32]{1,0:T(4,128)S(1)}, s32[4,32]{1,0:T(4,128)}, u32[]{:S(2)}) copy-start(s32[4,32]{1,0:T(4,128)} %param.16) | copy-start | bytes 1540
  143.6 133.6 %copy-start.1 = (f32[4,4096]{1,0:T(4,128)S(1)}, f32[4,4096]{1,0:T(4,128)}, u32[]{:S(2)}) copy-start(f32[4,4096]{1,0:T(4,128)} %param.11) | copy-start | bytes 196612
  143.6 133.6 %copy-start.2 = (f32[4,4096]{1,0:T(4,128)S(1)}, f32[4,4096]{1,0:T(4,128)}, u32[]{:S(2)}) copy-start(f32[4,4096]{1,0:T(4,128)} %param.13) | copy-start | bytes 196612
  143.6 133.6 %copy-start.3 = (f32[4,4096]{1,0:T(4,128)S(1)}, f32[4,4096]{1,0:T(4,128)}, u32[]{:S(2)}) copy-start(f32[4,4096]{1,0:T(4,128)} %param.14) | copy-start | bytes 196612
  143.7 122.1 %reduce-scatter.5.cloned.1.call-start = ((), (), s32[]{:S(2)}) async-start(), calls=%async_computation.6 | async-start | bytes 1310720 | tf_op jit(solution)/shard_map/reduce_scatter | solution.py:23
  267.6 9.2 %all-to-all-start = ((bf16[8,1,1,4,4096]{4,3,2,1,0:T(4,128)(2,1)}), bf16[8,1,1,4,4096]{4,3,2,1,0:T(4,128)(2,1)S(1)}, u32[]{:S(2)}, u32[]{:S(2)}) async-start(bf16[8,1,1,4,4096]{4,3,2,1,0:T(4,128)(2,1)} %copy.52), calls=%async_computation.2 | async-start | bytes 524288 | tf_op jit(solution)/shard_map/all_to_all | solution.py:34
  296.4 206.3 %all-to-all-start.2 = ((bf16[32,8,1,4,4096]{4,3,1,2,0:T(4,128)(2,1)}), bf16[32,8,1,4,4096]{4,3,1,2,0:T(4,128)(2,1)}, u32[]{:S(2)}, u32[]{:S(2)}) async-start(bf16[32,8,1,4,4096]{4,3,1,2,0:T(4,128)(2,1)} %stack.3), calls=%async_computation.4 | async-start | bytes 16777216 | tf_op jit(solution)/shard_map/all_to_all | solution.py:155
  306.7 196.0 %copy-start = (bf16[384,4096]{1,0:T(8,128)(2,1)S(1)}, bf16[384,4096]{1,0:T(8,128)(2,1)}, u32[]{:S(2)}) copy-start(bf16[384,4096]{1,0:T(8,128)(2,1)} %param.9) | copy-start | bytes 9437188
Sparse Core Ops, SparseCore 0:
  143.8 95.9 reduce-scatter.2
  242.4 23.3 reduce-scatter.4
